TPU v7x, 128 devices: a whole 4x4x4 slice. The times are simulated.
128 devices in a mesh: leaf: 128 (over y, z, x, core).
Axes of the slice: x: 4, y: 4, z: 4, core: 2. Of those that a mesh axis runs over, the one named last changes fastest.
Arguments:
- right_hand: float32 [2048, 32, 256], P('leaf')
- leaf_live: int32 [2048], P('leaf'), may hold values from 0 to 1, as said below
- near_index: int32 [2048, 6], P('leaf'), may hold values from 0 to 2047, as said below
- near_tile: bfloat16 [2048, 6, 256, 256], P('leaf'), may hold values from -1 to 5
- far_index: int32 [2048, 8], P('leaf'), may hold values from 0 to 2047, as said below
- far_couple: bfloat16 [2048, 8, 64, 64], P('leaf'), may hold values from -0.25 to 0.25
- leaf_basis: bfloat16 [2048, 64, 256], P('leaf'), may hold values from -0.375 to 0.375
- leaf_transfer: bfloat16 [2048, 64, 64], P('leaf'), may hold values from -0.1875 to 0.1875
- tree_up: bfloat16 [254, 64, 64], replicated, may hold values from -0.5 to 0.5
- tree_couple: bfloat16 [254, 64, 64], replicated, may hold values from -0.75 to 0.75
Outputs:
- basis_next: float32 [2048, 32, 256], P('leaf')
- hessenberg: float32 [6, 32], replicated
Inputs may be any that keep to these rules, and one draw needn't show every extreme that they name: `leaf_live`: each device's 16 slots hold between 5 and 16 live leaves, both counts reached on some device; which slots are live is arbitrary. `near_index`: entry 0 of each row is the row's own slot; every entry lies within 2 slots of its row's slot, and some entry lies exactly 2 away; entries may name dead slots. `far_index`: every entry lies within 16 slots of its row's slot, and some entry lies exactly 16 away; entries may name dead slots.
All inputs are finite; a program needn't handle non-finite values.
Results may differ from a plain program's by a relative error of at most 0.009.
Values may be sent and summed in bfloat16 or wider, within the bound.
No kernel may reach another device: no remote copies, remote signals or barrier semaphores. Data moves between devices by JAX's collectives and lax.ppermute only.
A program may use at most 128 MiB of HBM per device.

v0:
```python
import jax
import jax.numpy as jnp
from jax import lax
from jax.sharding import PartitionSpec as P

epsilon = 1e-06


def with_halo(array, sides, width):
    for axis, dim in sides:
        size, length = (lax.axis_size(axis), array.shape[dim])
        up = [(i, (i + 1) % size) for i in range(size - 1)]
        down = [(j, i) for i, j in up]
        last = lax.slice_in_dim(array, length - width, length, axis=dim)
        initial = lax.slice_in_dim(array, 0, width, axis=dim)
        before = lax.ppermute(last, axis, up)
        after = lax.ppermute(initial, axis, down)
        array = jnp.concatenate([before, array, after], axis=dim)
    return array


def swapped(array, axis, stride):
    return lax.ppermute(array, axis, [(i, i ^ 1 << stride) for i in range(lax.axis_size(axis))])


def apply_operator(
    vector,
    leaf_live,
    near_index,
    near_tile,
    far_index,
    far_couple,
    leaf_basis,
    leaf_transfer,
    tree_up,
    tree_couple,
):
    position = lax.axis_index("leaf")
    device_total = lax.axis_size("leaf")
    slot_count = vector.shape[0]
    live_mask = leaf_live.astype(jnp.float32)[:, None, None]
    inputs = (vector * live_mask).astype(jnp.bfloat16)
    padded = with_halo(inputs, (("leaf", 0),), slot_count)
    local_near = near_index - (position * slot_count - slot_count)
    columns = padded[local_near]
    near = jnp.einsum("inrp,inpq->irq", columns, near_tile, preferred_element_type=jnp.float32)
    moments = jnp.einsum(
        "irp,ikp->irk", inputs, leaf_basis, preferred_element_type=jnp.float32
    ).astype(jnp.bfloat16)
    moment_pad = with_halo(moments, (("leaf", 0),), slot_count)
    local_far = far_index - (position * slot_count - slot_count)
    far_term = jnp.einsum(
        "ifrk,ifkj->irj", moment_pad[local_far], far_couple, preferred_element_type=jnp.float32
    )
    box_moment = jnp.einsum(
        "irk,ikj->rj", moments, leaf_transfer, preferred_element_type=jnp.float32
    ).astype(jnp.bfloat16)
    levels = device_total.bit_length() - 1
    locals_list = []
    current = box_moment
    for level in range(levels):
        level_first = 2 * device_total - 2 * (device_total >> level)
        own_node = level_first + (position >> level)
        other_node = level_first + (position >> level ^ 1)
        sibling = swapped(current, "leaf", level)
        locals_list.append(
            jnp.dot(sibling, tree_couple[own_node], preferred_element_type=jnp.float32)
        )
        lifted = jnp.dot(current, tree_up[own_node], preferred_element_type=jnp.float32) + jnp.dot(
            sibling, tree_up[other_node], preferred_element_type=jnp.float32
        )
        current = lifted.astype(jnp.bfloat16)
    downward = jnp.zeros(box_moment.shape, jnp.bfloat16)
    for level in reversed(range(levels)):
        level_first = 2 * device_total - 2 * (device_total >> level)
        own_node = level_first + (position >> level)
        carried = jnp.einsum(
            "rj,kj->rk", downward, tree_up[own_node], preferred_element_type=jnp.float32
        )
        downward = (locals_list[level] + carried).astype(jnp.bfloat16)
    leaf_down = jnp.einsum(
        "rj,ikj->irk", downward, leaf_transfer, preferred_element_type=jnp.float32
    )
    local_total = (far_term + leaf_down).astype(jnp.bfloat16)
    spread = jnp.einsum("irk,ikp->irp", local_total, leaf_basis, preferred_element_type=jnp.float32)
    return live_mask * (near + spread)


def column_sums(first_field, second_field):
    return jnp.sum(first_field * second_field, axis=(0, 2))


def global_norm(field):
    return jnp.sqrt(lax.psum(column_sums(field, field), "leaf") + epsilon)


def inner_sums(stacked):
    return lax.psum(stacked, "leaf")


def on_device(
    right_hand,
    leaf_live,
    near_index,
    near_tile,
    far_index,
    far_couple,
    leaf_basis,
    leaf_transfer,
    tree_up,
    tree_couple,
):

    def operator(vector):
        return apply_operator(
            vector,
            leaf_live,
            near_index,
            near_tile,
            far_index,
            far_couple,
            leaf_basis,
            leaf_transfer,
            tree_up,
            tree_couple,
        )

    live_mask = leaf_live.astype(jnp.float32)[:, None, None]
    start_vec = right_hand * live_mask
    norm_start = global_norm(start_vec)
    basis_one = start_vec / norm_start[None, :, None]
    image_one = operator(basis_one)
    first_inner = inner_sums(column_sums(basis_one, image_one)[None])[0]
    residue_one = image_one - first_inner[None, :, None] * basis_one
    first_length = global_norm(residue_one)
    basis_two = residue_one / first_length[None, :, None]
    image_two = operator(basis_two)
    both_inner = inner_sums(
        jnp.stack([column_sums(basis_one, image_two), column_sums(basis_two, image_two)])
    )
    cross_inner = both_inner[0]
    self_inner = both_inner[1]
    residue_two = (
        image_two - cross_inner[None, :, None] * basis_one - self_inner[None, :, None] * basis_two
    )
    second_length = global_norm(residue_two)
    basis_next = residue_two / second_length[None, :, None]
    hessenberg = jnp.stack(
        [norm_start, first_inner, first_length, cross_inner, self_inner, second_length]
    )
    return (basis_next, hessenberg)


def solution(mesh):
    placed = (
        P("leaf", None, None),
        P("leaf"),
        P("leaf", None),
        P("leaf", None, None, None),
        P("leaf", None),
        P("leaf", None, None, None),
        P("leaf", None, None),
        P("leaf", None, None),
        P(),
        P(),
    )
    return jax.shard_map(
        on_device,
        mesh=mesh,
        in_specs=placed,
        out_specs=(P("leaf", None, None), P()),
        check_vma=False,
    )
```

profile of v0, /device:TPU:1, one launch (start us, length us, event | category | flops | bytes accessed | tf_op | source)
XLA Modules:
  0.0 563.7 jit_solution(7283835769958912221)
XLA Ops:
  2.7 68.7 %psum.35 = f32[32]{0:T(128)S(1)} all-reduce(f32[32]{0:T(128)S(1)} %multiply_reduce_fusion.5), channel_id=1, replica_groups=mesh['leaf'=128] {'leaf'}, use_global_device_ids=true, to_apply=%region_1.0 | all-reduce | flops 32 | bytes 256 | tf_op jit(solution)/shard_map/psum | solution.py:94
  75.2 2.6 collective-permute-start.2
  77.8 2.4 collective-permute-start.3
  80.2 3.2 collective-permute-start
  86.2 12.0 %constant_dynamic-slice_fusion.2 = (bf16[1,64,64]{0,2,1:T(8,128)(2,1)}, bf16[1,64,64]{0,2,1:T(8,128)(2,1)}, bf16[1,64,64]{0,2,1:T(8,128)(2,1)}, bf16[1,64,64]{0,...) fusion(bf16[254,64,64]{0,2,1:T(8,128)(2,1)} %param.18, ...), kind=kLoop, calls=%fused_computation.177 | loop fusion | bytes 213044 | tf_op jit(solution)/shard_map/dynamic_slice | solution.py:70
  103.8 9.0 %constant_dynamic-slice_fusion.19 = (bf16[1,64,64]{0,2,1:T(8,128)(2,1)S(1)}, bf16[1,64,64]{0,2,1:T(8,128)(2,1)}, bf16[1,64,64]{0,2,1:T(8,128)(2,1)}, bf16[1,64,6...) fusion(bf16[254,64,64]{0,2,1:T(8,128)(2,1)} %param.19, ...), kind=kLoop, calls=%fused_computation.194 | loop fusion | bytes 114716 | tf_op jit(solution)/shard_map/dynamic_slice | solution.py:67
  119.2 2.3 copy.42
  123.8 2.3 copy.45
  126.0 2.3 copy.47
  128.3 2.3 copy.48
  130.6 2.3 copy.50
  132.8 2.3 copy.51
  141.9 2.3 copy.57
  151.5 3.3 collective-permute-start.6
  156.7 4.8 collective-permute-start.7
  163.4 3.6 collective-permute-start.8
  168.9 5.7 %collective-permute-start.9 = (bf16[32,64]{1,0:T(8,128)(2,1)S(1)}, bf16[32,64]{1,0:T(8,128)(2,1)S(1)}, u32[]{:S(2)}, u32[]{:S(2)}) collective-permute-start(bf16[32,64]{1,0:T(8,128)(2,1)S(1)} %fusion.21), channel_id=1, source_target_pairs={{0,32},{1,33},{2,34},{3,35},{4,36},{5,37},{6,38},{7,39},{8,40},{9,... | collective-permute-start | bytes 12296 | tf_op jit(solution)/shard_map/ppermute | solution.py:23
  177.0 3.1 collective-permute-start.10
  181.4 2.3 copy.58
  183.6 2.3 copy.55
  185.9 2.3 copy.52
  190.4 2.3 copy.46
  211.0 3.0 gather_fusion
  214.0 8.1 %multiply_reduce_fusion.4 = (f32[32]{0:T(128)S(1)}, f32[16,32,256]{2,1,0:T(8,128)}) fusion(f32[32]{0:T(128)S(1)} %copy-done.19, f32[16,32,256]{2,1,0:T(8,128)S(1)} %copy-done.1, f32[16]{0:T(128)S(1)} %copy-done.11, f32[16,32,256]{2,1,0:T(8,128)} %fusion.9, bf16[16,6,32,256]{3,2,1,0:T(8,128)(2,1)} %bitcast.261, bf16[16,6,256,256]{3,2,1,0:T(8,128)(2,1)} %param.13), kind=kOutput, calls=%fused_computation.101 | convolution fusion | flops 403439584 | bytes 15728960 | tf_op jit(solution)/shard_map/inrp,inpq->irq/dot_general | solution.py:46
  222.2 67.2 %psum.36 = f32[1,32]{1,0:T(1,128)S(1)} all-reduce(f32[1,32]{1,0:T(1,128)S(1)} %bitcast.268), channel_id=1, replica_groups=mesh['leaf'=128] {'leaf'}, use_global_device_ids=true, to_apply=%region_3.0 | all-reduce | flops 32 | bytes 256 | tf_op jit(solution)/shard_map/psum | solution.py:98
  290.7 62.8 %psum.37 = f32[32]{0:T(128)S(1)} all-reduce(f32[32]{0:T(128)S(1)} %multiply_reduce_fusion.3), channel_id=1, replica_groups=mesh['leaf'=128] {'leaf'}, use_global_device_ids=true, to_apply=%region_5.0 | all-reduce | flops 32 | bytes 256 | tf_op jit(solution)/shard_map/psum | solution.py:94
  381.9 8.1 %collective-permute-start.11 = (bf16[16,32,256]{2,1,0:T(8,128)(2,1)}, bf16[16,32,256]{2,1,0:T(8,128)(2,1)}, u32[]{:S(2)}, u32[]{:S(2)}) collective-permute-start(bf16[16,32,256]{2,1,0:T(8,128)(2,1)} %get-tuple-element.6), channel_id=1, source_target_pairs={{0,1},{1,2},{2,3},{3,4},{4,5},{5,6},{6,7},{7,8},{8,9},{9,10},{10,1... | collective-permute-start | bytes 786440 | tf_op jit(solution)/shard_map/ppermute | solution.py:16
  391.9 3.6 collective-permute-start.13
  408.0 2.4 convolution_bitcast_fusion.3
  415.8 8.4 %multiply_reduce_fusion.2 = (f32[32]{0:T(128)S(1)}, f32[32]{0:T(128)S(1)}, f32[16,32,256]{2,1,0:T(8,128)}) fusion(f32[32]{0:T(128)S(1)} %copy-done.20, f32[16,32,256]{2,1,0:T(8,128)S(1)} %copy-done.1, f32[16]{0:T(128)S(1)} %copy-done.12, f32[16,32,256]{2,1,0:T(8,128)} %get-tuple-element.7, f32[16,32,256]{2,1,0:T(8,128)} %fusion.8, ...), kind=kOutput, calls=%fused_computation.97 | convolution fusion | flops 403701696 | bytes 16253376 | tf_op jit(solution)/shard_map/inrp,inpq->irq/dot_general | solution.py:46
  424.2 70.6 %psum.38 = f32[2,32]{1,0:T(2,128)S(1)} all-reduce(f32[2,32]{1,0:T(2,128)S(1)} %pad_maximum_fusion.4), channel_id=1, replica_groups=mesh['leaf'=128] {'leaf'}, use_global_device_ids=true, to_apply=%region_8.0 | all-reduce | flops 64 | bytes 512 | tf_op jit(solution)/shard_map/psum | solution.py:98
  497.0 64.1 %psum.39 = f32[32]{0:T(128)S(1)} all-reduce(f32[32]{0:T(128)S(1)} %get-tuple-element.4), channel_id=1, replica_groups=mesh['leaf'=128] {'leaf'}, use_global_device_ids=true, to_apply=%region_10.0 | all-reduce | flops 32 | bytes 256 | tf_op jit(solution)/shard_map/psum | solution.py:94
  (167 shorter events, 121.0 us)
Async XLA Ops:
  0.6 205.1 %copy-start = (bf16[16,8,64,64]{3,2,1,0:T(8,128)(2,1)S(1)}, bf16[16,8,64,64]{3,2,1,0:T(8,128)(2,1)}, u32[]{:S(2)}) copy-start(bf16[16,8,64,64]{3,2,1,0:T(8,128)(2,1)} %param.15) | copy-start | bytes 3145732
  0.6 84.7 %copy-start.4 = (bf16[16,64,64]{2,1,0:T(8,128)(2,1)S(1)}, bf16[16,64,64]{2,1,0:T(8,128)(2,1)}, u32[]{:S(2)}) copy-start(bf16[16,64,64]{2,1,0:T(8,128)(2,1)} %param.17) | copy-start | bytes 393220
  1.5 84.7 %copy-start.10 = (f32[16]{0:T(128)}, f32[16]{0:T(128)S(1)}, u32[]{:S(2)}) copy-start(f32[16]{0:T(128)S(1)} %convert_element_type.107) | copy-start | bytes 196
  75.2 127.6 %collective-permute-start.2 = (bf16[16,32,64]{2,1,0:T(8,128)(2,1)S(1)}, bf16[16,32,64]{2,1,0:T(8,128)(2,1)}, u32[]{:S(2)}, u32[]{:S(2)}) collective-permute-start(bf16[16,32,64]{2,1,0:T(8,128)(2,1)S(1)} %convolution_convert_fusion.1), channel_id=1, source_target_pairs={{0,1},{1,2},{2,3},{3,4},{4,5},{5,6},{6,7},{7,8},{8,9},{9,10},{10,1... | collective-permute-start | bytes 196616 | tf_op jit(solution)/shard_map/ppermute | solution.py:16
  77.8 125.0 %collective-permute-start.3 = (bf16[16,32,64]{2,1,0:T(8,128)(2,1)S(1)}, bf16[16,32,64]{2,1,0:T(8,128)(2,1)}, u32[]{:S(2)}, u32[]{:S(2)}) collective-permute-start(bf16[16,32,64]{2,1,0:T(8,128)(2,1)S(1)} %convolution_convert_fusion.1), channel_id=1, source_target_pairs={{1,0},{2,1},{3,2},{4,3},{5,4},{6,5},{7,6},{8,7},{9,8},{10,9},{11,1... | collective-permute-start | bytes 196616 | tf_op jit(solution)/shard_map/ppermute | solution.py:17
  80.2 128.6 %collective-permute-start = (bf16[16,32,256]{2,1,0:T(8,128)(2,1)}, bf16[16,32,256]{2,1,0:T(8,128)(2,1)}, u32[]{:S(2)}, u32[]{:S(2)}) collective-permute-start(bf16[16,32,256]{2,1,0:T(8,128)(2,1)} %multiply_convert_fusion.1), channel_id=1, source_target_pairs={{0,1},{1,2},{2,3},{3,4},{4,5},{5,6},{6,7},{7,8},{8,9},{9,10},{10,1... | collective-permute-start | bytes 786440 | tf_op jit(solution)/shard_map/ppermute | solution.py:16
  83.4 125.4 %collective-permute-start.1 = (bf16[16,32,256]{2,1,0:T(8,128)(2,1)}, bf16[16,32,256]{2,1,0:T(8,128)(2,1)}, u32[]{:S(2)}, u32[]{:S(2)}) collective-permute-start(bf16[16,32,256]{2,1,0:T(8,128)(2,1)} %multiply_convert_fusion.1), channel_id=1, source_target_pairs={{1,0},{2,1},{3,2},{4,3},{5,4},{6,5},{7,6},{8,7},{9,8},{10,9},{11,1... | collective-permute-start | bytes 786440 | tf_op jit(solution)/shard_map/ppermute | solution.py:17
  86.2 60.8 %collective-permute-start.4 = (bf16[32,64]{1,0:T(8,128)(2,1)}, bf16[32,64]{1,0:T(8,128)(2,1)}, u32[]{:S(2)}, u32[]{:S(2)}) collective-permute-start(bf16[32,64]{1,0:T(8,128)(2,1)} %fusion.10), channel_id=1, source_target_pairs={{0,1},{1,0},{2,3},{3,2},{4,5},{5,4},{6,7},{7,6},{8,9},{9,8},{10,11... | collective-permute-start | bytes 12296 | tf_op jit(solution)/shard_map/ppermute | solution.py:23
  147.8 2.9 collective-permute-start.5
  150.7 26.4 %copy-start.13 = (bf16[32,64]{1,0:T(8,128)(2,1)}, bf16[32,64]{1,0:T(8,128)(2,1)S(1)}, u32[]{:S(2)}) copy-start(bf16[32,64]{1,0:T(8,128)(2,1)S(1)} %collective-permute-done.5) | copy-start | bytes 12292
  151.5 4.4 collective-permute-start.6
  156.7 5.8 %collective-permute-start.7 = (bf16[32,64]{1,0:T(8,128)(2,1)S(1)}, bf16[32,64]{1,0:T(8,128)(2,1)S(1)}, u32[]{:S(2)}, u32[]{:S(2)}) collective-permute-start(bf16[32,64]{1,0:T(8,128)(2,1)S(1)} %fusion.17), channel_id=1, source_target_pairs={{0,8},{1,9},{2,10},{3,11},{4,12},{5,13},{6,14},{7,15},{8,0},{9,1},... | collective-permute-start | bytes 12296 | tf_op jit(solution)/shard_map/ppermute | solution.py:23
  163.4 4.6 collective-permute-start.8
  168.9 6.7 %collective-permute-start.9 = (bf16[32,64]{1,0:T(8,128)(2,1)S(1)}, bf16[32,64]{1,0:T(8,128)(2,1)S(1)}, u32[]{:S(2)}, u32[]{:S(2)}) collective-permute-start(bf16[32,64]{1,0:T(8,128)(2,1)S(1)} %fusion.21), channel_id=1, source_target_pairs={{0,32},{1,33},{2,34},{3,35},{4,36},{5,37},{6,38},{7,39},{8,40},{9,... | collective-permute-start | bytes 12296 | tf_op jit(solution)/shard_map/ppermute | solution.py:23
  177.0 19.0 %collective-permute-start.10 = (bf16[32,64]{1,0:T(8,128)(2,1)}, bf16[32,64]{1,0:T(8,128)(2,1)}, u32[]{:S(2)}, u32[]{:S(2)}) collective-permute-start(bf16[32,64]{1,0:T(8,128)(2,1)} %fusion.23), channel_id=1, source_target_pairs={{0,64},{1,65},{2,66},{3,67},{4,68},{5,69},{6,70},{7,71},{8,72},{9,... | collective-permute-start | bytes 12296 | tf_op jit(solution)/shard_map/ppermute | solution.py:23
  289.4 66.9 %copy-start.21 = (f32[1,32]{1,0:T(1,128)}, f32[1,32]{1,0:T(1,128)S(1)}, u32[]{:S(2)}) copy-start(f32[1,32]{1,0:T(1,128)S(1)} %psum.36) | copy-start | bytes 388
  357.5 46.9 %copy-start.6 = (bf16[16,32,64]{2,1,0:T(8,128)(2,1)}, bf16[16,32,64]{2,1,0:T(8,128)(2,1)S(1)}, u32[]{:S(2)}) copy-start(bf16[16,32,64]{2,1,0:T(8,128)(2,1)S(1)} %convolution_convert_fusion) | copy-start | bytes 196612
  357.7 1.5 collective-permute-start.15
  360.1 2.5 collective-permute-start.16
  363.5 4.0 collective-permute-start.17
  368.3 2.5 collective-permute-start.18
  371.6 4.1 collective-permute-start.19
  376.6 2.8 collective-permute-start.20
  380.2 17.5 %collective-permute-start.21 = (bf16[32,64]{1,0:T(8,128)(2,1)S(1)}, bf16[32,64]{1,0:T(8,128)(2,1)S(1)}, u32[]{:S(2)}, u32[]{:S(2)}) collective-permute-start(bf16[32,64]{1,0:T(8,128)(2,1)S(1)} %fusion.36), channel_id=1, source_target_pairs={{0,64},{1,65},{2,66},{3,67},{4,68},{5,69},{6,70},{7,71},{8,72},{9,... | collective-permute-start | bytes 12296 | tf_op jit(solution)/shard_map/ppermute | solution.py:23
  381.9 30.8 %collective-permute-start.11 = (bf16[16,32,256]{2,1,0:T(8,128)(2,1)}, bf16[16,32,256]{2,1,0:T(8,128)(2,1)}, u32[]{:S(2)}, u32[]{:S(2)}) collective-permute-start(bf16[16,32,256]{2,1,0:T(8,128)(2,1)} %get-tuple-element.6), channel_id=1, source_target_pairs={{0,1},{1,2},{2,3},{3,4},{4,5},{5,6},{6,7},{7,8},{8,9},{9,10},{10,1... | collective-permute-start | bytes 786440 | tf_op jit(solution)/shard_map/ppermute | solution.py:16
  390.0 22.7 %collective-permute-start.12 = (bf16[16,32,256]{2,1,0:T(8,128)(2,1)}, bf16[16,32,256]{2,1,0:T(8,128)(2,1)}, u32[]{:S(2)}, u32[]{:S(2)}) collective-permute-start(bf16[16,32,256]{2,1,0:T(8,128)(2,1)} %get-tuple-element.6), channel_id=1, source_target_pairs={{1,0},{2,1},{3,2},{4,3},{5,4},{6,5},{7,6},{8,7},{9,8},{10,9},{11,1... | collective-permute-start | bytes 786440 | tf_op jit(solution)/shard_map/ppermute | solution.py:17
  391.9 12.5 %collective-permute-start.13 = (bf16[16,32,64]{2,1,0:T(8,128)(2,1)S(1)}, bf16[16,32,64]{2,1,0:T(8,128)(2,1)S(1)}, u32[]{:S(2)}, u32[]{:S(2)}) collective-permute-start(bf16[16,32,64]{2,1,0:T(8,128)(2,1)S(1)} %convolution_convert_fusion), channel_id=1, source_target_pairs={{0,1},{1,2},{2,3},{3,4},{4,5},{5,6},{6,7},{7,8},{8,9},{9,10},{10,1... | collective-permute-start | bytes 196616 | tf_op jit(solution)/shard_map/ppermute | solution.py:16
  395.5 9.5 %collective-permute-start.14 = (bf16[16,32,64]{2,1,0:T(8,128)(2,1)S(1)}, bf16[16,32,64]{2,1,0:T(8,128)(2,1)}, u32[]{:S(2)}, u32[]{:S(2)}) collective-permute-start(bf16[16,32,64]{2,1,0:T(8,128)(2,1)S(1)} %convolution_convert_fusion), channel_id=1, source_target_pairs={{1,0},{2,1},{3,2},{4,3},{5,4},{6,5},{7,6},{8,7},{9,8},{10,9},{11,1... | collective-permute-start | bytes 196616 | tf_op jit(solution)/shard_map/ppermute | solution.py:17
  415.8 79.0 %copy-start.3 = (f32[16,32,256]{2,1,0:T(8,128)S(1)}, f32[16,32,256]{2,1,0:T(8,128)}, u32[]{:S(2)}) copy-start(f32[16,32,256]{2,1,0:T(8,128)} %get-tuple-element.7) | copy-start | bytes 1572868
  424.2 138.9 %copy-start.22 = (f32[1,32]{1,0:T(1,128)S(1)}, f32[1,32]{1,0:T(1,128)}, u32[]{:S(2)}) copy-start(f32[1,32]{1,0:T(1,128)} %copy-done.21) | copy-start | bytes 388
  424.2 138.9 %copy-start.23 = (f32[1,32]{1,0:T(1,128)S(1)}, f32[1,32]{1,0:T(1,128)}, u32[]{:S(2)}) copy-start(f32[1,32]{1,0:T(1,128)} %get-tuple-element.34) | copy-start | bytes 388
  424.2 138.9 %copy-start.24 = (f32[1,32]{1,0:T(1,128)S(1)}, f32[1,32]{1,0:T(1,128)}, u32[]{:S(2)}) copy-start(f32[1,32]{1,0:T(1,128)} %get-tuple-element.32) | copy-start | bytes 388
  (15 other events, 110.1 us)
where the time goes:
time: 570 us; the launch traced here: 564 us
  blocking collectives  333 us (58%)
  local copies, waits for them, and re-layouts  78.7 us (14%)
  matrix products  63.4 us (11%)
  starting transfers between devices  56.1 us (10%)
  other arithmetic  23.2 us (4%)
  waiting for transfers between devices  7.84 us (1%)
    psum x3, blocking collectives, global_norm(): return jnp.sqrt(lax.psum(column_sums(field, field), 'leaf') + epsilon)  196 us
    psum x2, blocking collectives, inner_sums(): return lax.psum(stacked, 'leaf')  138 us
    unnamed x70, local copies, waits for them, and re-layouts  43.1 us
    ppermute x14, starting transfers between devices, swapped(): lax.ppermute(array, axis, [(i, i ^ 1 << stride) for i in range(lax.axis_s...  30.2 us
    ppermute x4, starting transfers between devices, with_halo(): before = lax.ppermute(last, axis, up)  17.5 us
    dot_general x2, matrix products, apply_operator(): jnp.einsum('inrp,inpq->irq', columns, near_tile, preferred_element_type=j...  16.5 us
    dot_general x13, matrix products, apply_operator(): jnp.einsum('rj,kj->rk', downward, tree_up[own_node], preferred_element_ty...  13.2 us
    dynamic_slice x1, local copies, waits for them, and re-layouts, apply_operator(): tree_up[other_node]  12 us
  transfers between devices with their start and end apart: 22, of which 11 were waited for; matrix products, arithmetic and copies ran while one was open for 21% of the time, Pallas kernels for 0%

commit v1 on v0

--- a/solution.py
+++ b/solution.py
@@ -91,7 +91,7 @@
 
 
 def global_norm(field):
-    return jnp.sqrt(lax.psum(column_sums(field, field), "leaf") + epsilon)
+    return jnp.sqrt(jnp.sum(lax.all_gather(column_sums(field, field), "leaf"), axis=0) + epsilon)
 
 
 def inner_sums(stacked):

time: 570 us -> 571 us (level)
    unnamed x0 -> x3, blocking collectives: none -> 196 us
    psum x3 -> x0, blocking collectives: 196 us -> none  [global_norm(): return jnp.sqrt(lax.psum(column_sums(field, field), 'leaf') + epsilon)]
    unnamed x70 -> x76, local copies, waits for them, and re-layouts: 43.1 us -> 44 us
where the time goes in v1:
time: 571 us; the launch traced here: 565 us
  blocking collectives  334 us (58%)
  local copies, waits for them, and re-layouts  79.8 us (14%)
  matrix products  63.4 us (11%)
  starting transfers between devices  56 us (10%)
  other arithmetic  23.4 us (4%)
  waiting for transfers between devices  7.88 us (1%)
    unnamed x3, blocking collectives  196 us
    psum x2, blocking collectives, inner_sums(): return lax.psum(stacked, 'leaf')  138 us
    unnamed x76, local copies, waits for them, and re-layouts  44 us
    ppermute x14, starting transfers between devices, swapped(): lax.ppermute(array, axis, [(i, i ^ 1 << stride) for i in range(lax.axis_s...  30.2 us
    ppermute x4, starting transfers between devices, with_halo(): before = lax.ppermute(last, axis, up)  17.4 us
    dot_general x2, matrix products, apply_operator(): jnp.einsum('inrp,inpq->irq', columns, near_tile, preferred_element_type=j...  16.5 us
    dot_general x13, matrix products, apply_operator(): jnp.einsum('rj,kj->rk', downward, tree_up[own_node], preferred_element_ty...  13.2 us
    dynamic_slice x1, local copies, waits for them, and re-layouts, apply_operator(): tree_up[other_node]  12 us
  transfers between devices with their start and end apart: 22, of which 11 were waited for; matrix products, arithmetic and copies ran while one was open for 21% of the time, Pallas kernels for 0%

profile of v1, /device:TPU:1, one launch (start us, length us, event | category | flops | bytes accessed | tf_op | source)
XLA Modules:
  0.0 565.2 jit_solution(12844319850355305371)
XLA Ops:
  3.0 68.7 %all-reduce = f32[4096]{0:T(1024)S(1)} all-reduce(f32[4096]{0:T(1024)S(1)} %dynamic-update-slice), channel_id=2, replica_groups=mesh['leaf'=128] {'leaf'}, use_global_device_ids=true, to_apply=%add | all-reduce | flops 4096 | bytes 32768
  75.7 2.6 collective-permute-start.2
  78.3 2.4 collective-permute-start.3
  80.7 3.2 collective-permute-start
  86.6 12.0 %constant_dynamic-slice_fusion.2 = (bf16[1,64,64]{0,2,1:T(8,128)(2,1)}, bf16[1,64,64]{0,2,1:T(8,128)(2,1)}, bf16[1,64,64]{0,2,1:T(8,128)(2,1)}, bf16[1,64,64]{0,...) fusion(bf16[254,64,64]{0,2,1:T(8,128)(2,1)} %param.18, ...), kind=kLoop, calls=%fused_computation.177 | loop fusion | bytes 213044 | tf_op jit(solution)/shard_map/dynamic_slice | solution.py:70
  104.2 9.0 %constant_dynamic-slice_fusion.19 = (bf16[1,64,64]{0,2,1:T(8,128)(2,1)S(1)}, bf16[1,64,64]{0,2,1:T(8,128)(2,1)}, bf16[1,64,64]{0,2,1:T(8,128)(2,1)}, bf16[1,64,6...) fusion(bf16[254,64,64]{0,2,1:T(8,128)(2,1)} %param.19, ...), kind=kLoop, calls=%fused_computation.194 | loop fusion | bytes 114716 | tf_op jit(solution)/shard_map/dynamic_slice | solution.py:67
  119.6 2.3 copy.42
  126.4 2.3 copy.47
  128.7 2.3 copy.48
  131.0 2.3 copy.50
  133.2 2.3 copy.51
  135.5 2.3 copy.53
  140.1 2.3 copy.56
  151.9 3.4 collective-permute-start.6
  157.1 4.8 collective-permute-start.7
  163.8 3.7 collective-permute-start.8
  169.4 5.7 %collective-permute-start.9 = (bf16[32,64]{1,0:T(8,128)(2,1)S(1)}, bf16[32,64]{1,0:T(8,128)(2,1)S(1)}, u32[]{:S(2)}, u32[]{:S(2)}) collective-permute-start(bf16[32,64]{1,0:T(8,128)(2,1)S(1)} %fusion.21), channel_id=1, source_target_pairs={{0,32},{1,33},{2,34},{3,35},{4,36},{5,37},{6,38},{7,39},{8,40},{9,... | collective-permute-start | bytes 12296 | tf_op jit(solution)/shard_map/ppermute | solution.py:23
  177.5 3.0 collective-permute-start.10
  181.8 2.3 copy.58
  184.1 2.3 copy.55
  188.6 2.3 copy.49
  190.9 2.3 copy.46
  211.4 3.1 gather_fusion
  214.5 8.1 %multiply_reduce_fusion.4 = (f32[32]{0:T(128)S(1)}, f32[16,32,256]{2,1,0:T(8,128)}) fusion(f32[32]{0:T(128)S(1)} %copy-done.19, f32[16,32,256]{2,1,0:T(8,128)S(1)} %copy-done.1, f32[16]{0:T(128)S(1)} %copy-done.11, f32[16,32,256]{2,1,0:T(8,128)} %fusion.9, bf16[16,6,32,256]{3,2,1,0:T(8,128)(2,1)} %bitcast.261, bf16[16,6,256,256]{3,2,1,0:T(8,128)(2,1)} %param.13), kind=kOutput, calls=%fused_computation.101 | convolution fusion | flops 403439584 | bytes 15728960 | tf_op jit(solution)/shard_map/inrp,inpq->irq/dot_general | solution.py:46
  222.6 67.2 %psum.14 = f32[1,32]{1,0:T(1,128)S(1)} all-reduce(f32[1,32]{1,0:T(1,128)S(1)} %bitcast.268), channel_id=1, replica_groups=mesh['leaf'=128] {'leaf'}, use_global_device_ids=true, to_apply=%region_3.0 | all-reduce | flops 32 | bytes 256 | tf_op jit(solution)/shard_map/psum | solution.py:98
  291.5 63.0 %all-reduce.1 = f32[4096]{0:T(1024)S(1)} all-reduce(f32[4096]{0:T(1024)S(1)} %dynamic-update-slice.1), channel_id=3, replica_groups=mesh['leaf'=128] {'leaf'}, use_global_device_ids=true, to_apply=%add.1 | all-reduce | flops 4096 | bytes 32768
  382.9 8.1 %collective-permute-start.11 = (bf16[16,32,256]{2,1,0:T(8,128)(2,1)}, bf16[16,32,256]{2,1,0:T(8,128)(2,1)}, u32[]{:S(2)}, u32[]{:S(2)}) collective-permute-start(bf16[16,32,256]{2,1,0:T(8,128)(2,1)} %get-tuple-element.6), channel_id=1, source_target_pairs={{0,1},{1,2},{2,3},{3,4},{4,5},{5,6},{6,7},{7,8},{8,9},{9,10},{10,1... | collective-permute-start | bytes 786440 | tf_op jit(solution)/shard_map/ppermute | solution.py:16
  392.9 3.6 collective-permute-start.13
  409.0 2.4 convolution_bitcast_fusion.3
  416.8 8.4 %multiply_reduce_fusion.2 = (f32[32]{0:T(128)S(1)}, f32[32]{0:T(128)S(1)}, f32[16,32,256]{2,1,0:T(8,128)}) fusion(f32[32]{0:T(128)S(1)} %copy-done.20, f32[16,32,256]{2,1,0:T(8,128)S(1)} %copy-done.1, f32[16]{0:T(128)S(1)} %copy-done.12, f32[16,32,256]{2,1,0:T(8,128)} %get-tuple-element.7, f32[16,32,256]{2,1,0:T(8,128)} %fusion.8, ...), kind=kOutput, calls=%fused_computation.97 | convolution fusion | flops 403701696 | bytes 16253376 | tf_op jit(solution)/shard_map/inrp,inpq->irq/dot_general | solution.py:46
  425.2 70.7 %psum.15 = f32[2,32]{1,0:T(2,128)S(1)} all-reduce(f32[2,32]{1,0:T(2,128)S(1)} %pad_maximum_fusion.4), channel_id=1, replica_groups=mesh['leaf'=128] {'leaf'}, use_global_device_ids=true, to_apply=%region_8.0 | all-reduce | flops 64 | bytes 512 | tf_op jit(solution)/shard_map/psum | solution.py:98
  498.4 64.2 %all-reduce.2 = f32[4096]{0:T(1024)S(1)} all-reduce(f32[4096]{0:T(1024)S(1)} %dynamic-update-slice.2), channel_id=4, replica_groups=mesh['leaf'=128] {'leaf'}, use_global_device_ids=true, to_apply=%add.2 | all-reduce | flops 4096 | bytes 32768
  (179 shorter events, 122.2 us)
Async XLA Ops:
  0.6 205.6 %copy-start = (bf16[16,8,64,64]{3,2,1,0:T(8,128)(2,1)S(1)}, bf16[16,8,64,64]{3,2,1,0:T(8,128)(2,1)}, u32[]{:S(2)}) copy-start(bf16[16,8,64,64]{3,2,1,0:T(8,128)(2,1)} %param.15) | copy-start | bytes 3145732
  0.6 85.1 %copy-start.4 = (bf16[16,64,64]{2,1,0:T(8,128)(2,1)S(1)}, bf16[16,64,64]{2,1,0:T(8,128)(2,1)}, u32[]{:S(2)}) copy-start(bf16[16,64,64]{2,1,0:T(8,128)(2,1)} %param.17) | copy-start | bytes 393220
  1.5 85.1 %copy-start.10 = (f32[16]{0:T(128)}, f32[16]{0:T(128)S(1)}, u32[]{:S(2)}) copy-start(f32[16]{0:T(128)S(1)} %convert_element_type.107) | copy-start | bytes 196
  75.7 127.6 %collective-permute-start.2 = (bf16[16,32,64]{2,1,0:T(8,128)(2,1)S(1)}, bf16[16,32,64]{2,1,0:T(8,128)(2,1)}, u32[]{:S(2)}, u32[]{:S(2)}) collective-permute-start(bf16[16,32,64]{2,1,0:T(8,128)(2,1)S(1)} %convolution_convert_fusion.1), channel_id=1, source_target_pairs={{0,1},{1,2},{2,3},{3,4},{4,5},{5,6},{6,7},{7,8},{8,9},{9,10},{10,1... | collective-permute-start | bytes 196616 | tf_op jit(solution)/shard_map/ppermute | solution.py:16
  78.3 125.1 %collective-permute-start.3 = (bf16[16,32,64]{2,1,0:T(8,128)(2,1)S(1)}, bf16[16,32,64]{2,1,0:T(8,128)(2,1)}, u32[]{:S(2)}, u32[]{:S(2)}) collective-permute-start(bf16[16,32,64]{2,1,0:T(8,128)(2,1)S(1)} %convolution_convert_fusion.1), channel_id=1, source_target_pairs={{1,0},{2,1},{3,2},{4,3},{5,4},{6,5},{7,6},{8,7},{9,8},{10,9},{11,1... | collective-permute-start | bytes 196616 | tf_op jit(solution)/shard_map/ppermute | solution.py:17
  80.7 128.6 %collective-permute-start = (bf16[16,32,256]{2,1,0:T(8,128)(2,1)}, bf16[16,32,256]{2,1,0:T(8,128)(2,1)}, u32[]{:S(2)}, u32[]{:S(2)}) collective-permute-start(bf16[16,32,256]{2,1,0:T(8,128)(2,1)} %multiply_convert_fusion.1), channel_id=1, source_target_pairs={{0,1},{1,2},{2,3},{3,4},{4,5},{5,6},{6,7},{7,8},{8,9},{9,10},{10,1... | collective-permute-start | bytes 786440 | tf_op jit(solution)/shard_map/ppermute | solution.py:16
  83.9 125.4 %collective-permute-start.1 = (bf16[16,32,256]{2,1,0:T(8,128)(2,1)}, bf16[16,32,256]{2,1,0:T(8,128)(2,1)}, u32[]{:S(2)}, u32[]{:S(2)}) collective-permute-start(bf16[16,32,256]{2,1,0:T(8,128)(2,1)} %multiply_convert_fusion.1), channel_id=1, source_target_pairs={{1,0},{2,1},{3,2},{4,3},{5,4},{6,5},{7,6},{8,7},{9,8},{10,9},{11,1... | collective-permute-start | bytes 786440 | tf_op jit(solution)/shard_map/ppermute | solution.py:17
  86.6 60.7 %collective-permute-start.4 = (bf16[32,64]{1,0:T(8,128)(2,1)}, bf16[32,64]{1,0:T(8,128)(2,1)}, u32[]{:S(2)}, u32[]{:S(2)}) collective-permute-start(bf16[32,64]{1,0:T(8,128)(2,1)} %fusion.10), channel_id=1, source_target_pairs={{0,1},{1,0},{2,3},{3,2},{4,5},{5,4},{6,7},{7,6},{8,9},{9,8},{10,11... | collective-permute-start | bytes 12296 | tf_op jit(solution)/shard_map/ppermute | solution.py:23
  148.2 2.8 collective-permute-start.5
  151.0 26.5 %copy-start.13 = (bf16[32,64]{1,0:T(8,128)(2,1)}, bf16[32,64]{1,0:T(8,128)(2,1)S(1)}, u32[]{:S(2)}) copy-start(bf16[32,64]{1,0:T(8,128)(2,1)S(1)} %collective-permute-done.5) | copy-start | bytes 12292
  151.9 4.4 collective-permute-start.6
  157.1 5.8 %collective-permute-start.7 = (bf16[32,64]{1,0:T(8,128)(2,1)S(1)}, bf16[32,64]{1,0:T(8,128)(2,1)S(1)}, u32[]{:S(2)}, u32[]{:S(2)}) collective-permute-start(bf16[32,64]{1,0:T(8,128)(2,1)S(1)} %fusion.17), channel_id=1, source_target_pairs={{0,8},{1,9},{2,10},{3,11},{4,12},{5,13},{6,14},{7,15},{8,0},{9,1},... | collective-permute-start | bytes 12296 | tf_op jit(solution)/shard_map/ppermute | solution.py:23
  163.8 4.8 collective-permute-start.8
  169.4 6.7 %collective-permute-start.9 = (bf16[32,64]{1,0:T(8,128)(2,1)S(1)}, bf16[32,64]{1,0:T(8,128)(2,1)S(1)}, u32[]{:S(2)}, u32[]{:S(2)}) collective-permute-start(bf16[32,64]{1,0:T(8,128)(2,1)S(1)} %fusion.21), channel_id=1, source_target_pairs={{0,32},{1,33},{2,34},{3,35},{4,36},{5,37},{6,38},{7,39},{8,40},{9,... | collective-permute-start | bytes 12296 | tf_op jit(solution)/shard_map/ppermute | solution.py:23
  177.5 19.0 %collective-permute-start.10 = (bf16[32,64]{1,0:T(8,128)(2,1)}, bf16[32,64]{1,0:T(8,128)(2,1)}, u32[]{:S(2)}, u32[]{:S(2)}) collective-permute-start(bf16[32,64]{1,0:T(8,128)(2,1)} %fusion.23), channel_id=1, source_target_pairs={{0,64},{1,65},{2,66},{3,67},{4,68},{5,69},{6,70},{7,71},{8,72},{9,... | collective-permute-start | bytes 12296 | tf_op jit(solution)/shard_map/ppermute | solution.py:23
  289.9 67.5 %copy-start.21 = (f32[1,32]{1,0:T(1,128)}, f32[1,32]{1,0:T(1,128)S(1)}, u32[]{:S(2)}) copy-start(f32[1,32]{1,0:T(1,128)S(1)} %psum.14) | copy-start | bytes 388
  358.5 46.9 %copy-start.6 = (bf16[16,32,64]{2,1,0:T(8,128)(2,1)}, bf16[16,32,64]{2,1,0:T(8,128)(2,1)S(1)}, u32[]{:S(2)}) copy-start(bf16[16,32,64]{2,1,0:T(8,128)(2,1)S(1)} %convolution_convert_fusion) | copy-start | bytes 196612
  358.8 1.5 collective-permute-start.15
  361.1 2.5 collective-permute-start.16
  364.5 4.0 collective-permute-start.17
  369.3 2.5 collective-permute-start.18
  372.7 4.1 collective-permute-start.19
  377.6 2.8 collective-permute-start.20
  381.2 17.5 %collective-permute-start.21 = (bf16[32,64]{1,0:T(8,128)(2,1)S(1)}, bf16[32,64]{1,0:T(8,128)(2,1)S(1)}, u32[]{:S(2)}, u32[]{:S(2)}) collective-permute-start(bf16[32,64]{1,0:T(8,128)(2,1)S(1)} %fusion.36), channel_id=1, source_target_pairs={{0,64},{1,65},{2,66},{3,67},{4,68},{5,69},{6,70},{7,71},{8,72},{9,... | collective-permute-start | bytes 12296 | tf_op jit(solution)/shard_map/ppermute | solution.py:23
  382.9 30.8 %collective-permute-start.11 = (bf16[16,32,256]{2,1,0:T(8,128)(2,1)}, bf16[16,32,256]{2,1,0:T(8,128)(2,1)}, u32[]{:S(2)}, u32[]{:S(2)}) collective-permute-start(bf16[16,32,256]{2,1,0:T(8,128)(2,1)} %get-tuple-element.6), channel_id=1, source_target_pairs={{0,1},{1,2},{2,3},{3,4},{4,5},{5,6},{6,7},{7,8},{8,9},{9,10},{10,1... | collective-permute-start | bytes 786440 | tf_op jit(solution)/shard_map/ppermute | solution.py:16
  391.0 22.7 %collective-permute-start.12 = (bf16[16,32,256]{2,1,0:T(8,128)(2,1)}, bf16[16,32,256]{2,1,0:T(8,128)(2,1)}, u32[]{:S(2)}, u32[]{:S(2)}) collective-permute-start(bf16[16,32,256]{2,1,0:T(8,128)(2,1)} %get-tuple-element.6), channel_id=1, source_target_pairs={{1,0},{2,1},{3,2},{4,3},{5,4},{6,5},{7,6},{8,7},{9,8},{10,9},{11,1... | collective-permute-start | bytes 786440 | tf_op jit(solution)/shard_map/ppermute | solution.py:17
  392.9 12.5 %collective-permute-start.13 = (bf16[16,32,64]{2,1,0:T(8,128)(2,1)S(1)}, bf16[16,32,64]{2,1,0:T(8,128)(2,1)S(1)}, u32[]{:S(2)}, u32[]{:S(2)}) collective-permute-start(bf16[16,32,64]{2,1,0:T(8,128)(2,1)S(1)} %convolution_convert_fusion), channel_id=1, source_target_pairs={{0,1},{1,2},{2,3},{3,4},{4,5},{5,6},{6,7},{7,8},{8,9},{9,10},{10,1... | collective-permute-start | bytes 196616 | tf_op jit(solution)/shard_map/ppermute | solution.py:16
  396.5 9.5 %collective-permute-start.14 = (bf16[16,32,64]{2,1,0:T(8,128)(2,1)S(1)}, bf16[16,32,64]{2,1,0:T(8,128)(2,1)}, u32[]{:S(2)}, u32[]{:S(2)}) collective-permute-start(bf16[16,32,64]{2,1,0:T(8,128)(2,1)S(1)} %convolution_convert_fusion), channel_id=1, source_target_pairs={{1,0},{2,1},{3,2},{4,3},{5,4},{6,5},{7,6},{8,7},{9,8},{10,9},{11,1... | collective-permute-start | bytes 196616 | tf_op jit(solution)/shard_map/ppermute | solution.py:17
  416.8 79.1 %copy-start.3 = (f32[16,32,256]{2,1,0:T(8,128)S(1)}, f32[16,32,256]{2,1,0:T(8,128)}, u32[]{:S(2)}) copy-start(f32[16,32,256]{2,1,0:T(8,128)} %get-tuple-element.7) | copy-start | bytes 1572868
  425.2 139.4 %copy-start.22 = (f32[1,32]{1,0:T(1,128)S(1)}, f32[1,32]{1,0:T(1,128)}, u32[]{:S(2)}) copy-start(f32[1,32]{1,0:T(1,128)} %copy-done.21) | copy-start | bytes 388
  425.2 139.4 %copy-start.23 = (f32[1,32]{1,0:T(1,128)S(1)}, f32[1,32]{1,0:T(1,128)}, u32[]{:S(2)}) copy-start(f32[1,32]{1,0:T(1,128)} %get-tuple-element.34) | copy-start | bytes 388
  425.2 139.4 %copy-start.24 = (f32[1,32]{1,0:T(1,128)S(1)}, f32[1,32]{1,0:T(1,128)}, u32[]{:S(2)}) copy-start(f32[1,32]{1,0:T(1,128)} %get-tuple-element.32) | copy-start | bytes 388
  (15 other events, 110.0 us)
